TPU v7x, 32 devices: a whole 2x2x4 slice. The times are simulated.
32 devices in a mesh: gx: 8 (over z, core), gy: 4 (over y, x).
Axes of the slice: x: 2, y: 2, z: 4, core: 2. Of those that a mesh axis runs over, the one named last changes fastest.
Arguments:
- displacement: float32 [3, 64, 32, 128], P(None, 'gx', 'gy'), may hold values from -6 to 6
- velocity: float32 [3, 64, 32, 128], P(None, 'gx', 'gy'), may hold values from -6 to 6
- region: int32 [64, 32, 128], P('gx', 'gy'), may hold values from 0 to 3
- bond_words: int32 [11, 64, 32, 128], P(None, 'gx', 'gy'), may hold values from 0 to 4095, as said below
- moduli: float32 [3, 4], replicated, may hold values from 0.5 to 2
Outputs:
- new_displacement: float32 [3, 64, 32, 128], P(None, 'gx', 'gy')
- new_velocity: float32 [3, 64, 32, 128], P(None, 'gx', 'gy')
Inputs may be any that keep to these rules, and one draw needn't show every extreme that they name: `bond_words`: bonds are the integer offsets (a, b, c) with 0 < a*a + b*b + c*c <= 9, numbered 0 to 121 in increasing lexicographic order. Bond q of a node is bit q % 12 of word q // 12 (bit 0 the lowest); a set bit means the bond is intact. A bond whose far end lies outside the grid is never intact; the six bonds of length one are intact wherever they stay inside the grid; bond q of node p equals bond 121 - q of node p + xi_q.
All inputs are finite; a program needn't handle non-finite values.
Results may differ from a plain program's by a relative error of at most 0.00002.
Values sent between devices are 32-bit elements; how exact they have to be, the bound alone decides.
A program may use at most 64 MiB of HBM per device.

v0:
```python
import math

import jax
import jax.numpy as jnp
from jax import lax
from jax.sharding import PartitionSpec as P

HORIZON = 3


time_step = 0.3
bits_per_word = 12


def extended(x, sides, width):
    for axis, dim in sides:
        size, length = (lax.axis_size(axis), x.shape[dim])
        up = [(i, (i + 1) % size) for i in range(size - 1)]
        down = [(j, i) for i, j in up]
        last = lax.slice_in_dim(x, length - width, length, axis=dim)
        first = lax.slice_in_dim(x, 0, width, axis=dim)
        before = lax.ppermute(last, axis, up)
        after = lax.ppermute(first, axis, down)
        x = jnp.concatenate([before, x, after], axis=dim)
    return x


def bond_offsets():
    listed = []
    for shift_x in range(-HORIZON, HORIZON + 1):
        for shift_y in range(-HORIZON, HORIZON + 1):
            for shift_z in range(-HORIZON, HORIZON + 1):
                radius = shift_x * shift_x + shift_y * shift_y + shift_z * shift_z
                if 0 < radius <= HORIZON * HORIZON:
                    listed.append((shift_x, shift_y, shift_z))
    return listed


def bond_length(offset):
    return math.sqrt(offset[0] * offset[0] + offset[1] * offset[1] + offset[2] * offset[2])


def bond_bit(bond_words, number):
    word_index = number // bits_per_word
    bit_shift = number % bits_per_word
    return jnp.bitwise_and(jnp.right_shift(bond_words[word_index], bit_shift), 1).astype(
        jnp.float32
    )


def materials(region, moduli):
    fields = jnp.zeros((3,) + region.shape, jnp.float32)
    for material in range(moduli.shape[1]):
        fields = jnp.where(
            (region == material)[None], moduli[:, material][:, None, None, None], fields
        )
    return (fields[0], fields[1], fields[2])


def window(padded, offset, block_shape):
    start_x = HORIZON + offset[0]
    start_y = HORIZON + offset[1]
    start_z = HORIZON + offset[2]
    return padded[
        ...,
        start_x : start_x + block_shape[0],
        start_y : start_y + block_shape[1],
        start_z : start_z + block_shape[2],
    ]


def stretch_of(padded, centre, offset):
    length = bond_length(offset)
    block_shape = centre.shape[1:]
    start_x = HORIZON + offset[0]
    start_y = HORIZON + offset[1]
    start_z = HORIZON + offset[2]
    along = None
    for position in range(3):
        if offset[position] != 0:
            neighbour = padded[
                position,
                start_x : start_x + block_shape[0],
                start_y : start_y + block_shape[1],
                start_z : start_z + block_shape[2],
            ]
            term = (neighbour - centre[position]) * (offset[position] / length)
            along = term if along is None else along + term
    return along


def pad_depth(field):
    margins = ((0, 0),) * (field.ndim - 1) + ((HORIZON, HORIZON),)
    return jnp.pad(field, margins)


def on_device(displacement, velocity, region, bond_words, moduli):
    offsets = bond_offsets()
    block_shape = region.shape
    bulk_modulus, shear_modulus, density = materials(region, moduli)
    volume = jnp.zeros(block_shape, jnp.float32)
    for number, offset in enumerate(offsets):
        volume = volume + bond_bit(bond_words, number) * bond_length(offset)
    pressure_ratio = (3.0 * bulk_modulus - 5.0 * shear_modulus) / volume
    shear_term = 15.0 * shear_modulus / volume
    inverse_mass = 1.0 / density
    shear_padded = pad_depth(extended(shear_term, (("gx", 0), ("gy", 1)), HORIZON))
    imbalance = [jnp.zeros(block_shape, jnp.float32) for position in range(3)]
    for number, offset in enumerate(offsets):
        intact = bond_bit(bond_words, number)
        length = bond_length(offset)
        for position in range(3):
            if offset[position] != 0:
                imbalance[position] = imbalance[position] + intact * (offset[position] / length)
    padded = extended(displacement, (("gx", 1), ("gy", 2)), HORIZON)
    padded = pad_depth(padded)
    accumulated = jnp.zeros(block_shape, jnp.float32)
    shear_pull = [jnp.zeros(block_shape, jnp.float32) for position in range(3)]
    for number, offset in enumerate(offsets):
        intact = bond_bit(bond_words, number)
        length = bond_length(offset)
        weighted = intact * stretch_of(padded, displacement, offset)
        accumulated = accumulated + weighted
        for position in range(3):
            if offset[position] != 0:
                shear_pull[position] = shear_pull[position] + weighted * (
                    offset[position] / (length * length)
                )
    dilatation = 3.0 * accumulated / volume
    pressure_term = dilatation * pressure_ratio
    pressure_padded = pad_depth(extended(pressure_term, (("gx", 0), ("gy", 1)), HORIZON))
    force_parts = [jnp.zeros(block_shape, jnp.float32) for position in range(3)]
    for number, offset in enumerate(offsets):
        length = bond_length(offset)
        stretch = stretch_of(padded, displacement, offset)
        coefficient = bond_bit(bond_words, number) * (
            window(pressure_padded, offset, block_shape)
            + window(shear_padded, offset, block_shape) * stretch * (1.0 / length)
        )
        for position in range(3):
            if offset[position] != 0:
                force_parts[position] = force_parts[position] + coefficient * (
                    offset[position] / length
                )
    for position in range(3):
        force_parts[position] = (
            force_parts[position]
            + pressure_term * imbalance[position]
            + shear_term * shear_pull[position]
        )
    force_sum = jnp.stack(force_parts)
    velocity = velocity + time_step * force_sum * inverse_mass
    displacement = displacement + time_step * velocity
    return (displacement, velocity)


def solution(mesh):
    placed = (
        P(None, "gx", "gy", None),
        P(None, "gx", "gy", None),
        P("gx", "gy", None),
        P(None, "gx", "gy", None),
        P(),
    )
    return jax.shard_map(
        on_device,
        mesh=mesh,
        in_specs=placed,
        out_specs=(P(None, "gx", "gy", None), P(None, "gx", "gy", None)),
        check_vma=False,
    )
```

profile of v0, /device:TPU:10, one launch (start us, length us, event | category | flops | bytes accessed | tf_op | source)
XLA Modules:
  0.0 61.6 jit_solution(15914673315717490520)
XLA Ops:
  0.6 0.8 %fusion.1691 = (f32[3,3,8,128]{3,2,1,0:T(8,128)S(1)}, f32[3,3,8,128]{3,2,1,0:T(8,128)S(1)}) fusion(f32[3,8,8,128]{3,2,1,0:T(8,128)} %param.5), kind=kLoop, calls=%fused_computation.2651 | loop fusion | bytes 147456 | tf_op jit(solution)/shard_map/slice | solution.py:21
  1.4 1.9 %collective-permute-start = (f32[3,3,8,128]{3,2,1,0:T(8,128)S(1)}, f32[3,3,8,128]{3,2,1,0:T(8,128)S(1)}, u32[]{:S(2)}, u32[]{:S(2)}) collective-permute-start(f32[3,3,8,128]{3,2,1,0:T(8,128)S(1)} %get-tuple-element.190), channel_id=1, source_target_pairs={{0,4},{4,8},{8,12},{12,16},{16,20},{20,24},{24,28},{1,5},{5,9},{9,... | collective-permute-start | bytes 110600 | tf_op jit(solution)/shard_map/ppermute | solution.py:22
  3.4 3.6 %collective-permute-start.1 = (f32[3,3,8,128]{3,2,1,0:T(8,128)S(1)}, f32[3,3,8,128]{3,2,1,0:T(8,128)S(1)}, u32[]{:S(2)}, u32[]{:S(2)}) collective-permute-start(f32[3,3,8,128]{3,2,1,0:T(8,128)S(1)} %get-tuple-element.189), channel_id=1, source_target_pairs={{4,0},{8,4},{12,8},{16,12},{20,16},{24,20},{28,24},{5,1},{9,5},{13... | collective-permute-start | bytes 110600 | tf_op jit(solution)/shard_map/ppermute | solution.py:23
  7.1 0.6 %copy-done.3 = f32[3,4]{1,0:T(4,128)S(1)} copy-done((f32[3,4]{1,0:T(4,128)S(1)}, f32[3,4]{1,0:T(4,128)}, u32[]{:S(2)}) %copy-start.3) | copy-done | bytes 72
  7.7 0.2 slice_reduce_fusion.3
  8.0 0.8 %copy-done.1 = f32[3,8,8,128]{3,2,1,0:T(8,128)S(1)} copy-done((f32[3,8,8,128]{3,2,1,0:T(8,128)S(1)}, f32[3,8,8,128]{3,2,1,0:T(8,128)}, u32[]{:S(2)}) %copy-start.1) | copy-done | bytes 98328
  8.9 3.4 %collective-permute-start.2 = (f32[3,14,3,128]{3,2,1,0:T(4,128)S(1)}, f32[3,14,3,128]{3,2,1,0:T(4,128)S(1)}, u32[]{:S(2)}, u32[]{:S(2)}) collective-permute-start(f32[3,14,3,128]{3,2,1,0:T(4,128)S(1)} %get-tuple-element.184), channel_id=1, source_target_pairs={{0,1},{1,2},{2,3},{4,5},{5,6},{6,7},{8,9},{9,10},{10,11},{12,13},{... | collective-permute-start | bytes 193544 | tf_op jit(solution)/shard_map/ppermute | solution.py:22
  12.3 2.4 %collective-permute-start.3 = (f32[3,14,3,128]{3,2,1,0:T(4,128)S(1)}, f32[3,14,3,128]{3,2,1,0:T(4,128)S(1)}, u32[]{:S(2)}, u32[]{:S(2)}) collective-permute-start(f32[3,14,3,128]{3,2,1,0:T(4,128)S(1)} %get-tuple-element.185), channel_id=1, source_target_pairs={{1,0},{2,1},{3,2},{5,4},{6,5},{7,6},{9,8},{10,9},{11,10},{13,12},{... | collective-permute-start | bytes 193544 | tf_op jit(solution)/shard_map/ppermute | solution.py:23
  14.8 0.9 %collective-permute-done.2 = f32[3,14,3,128]{3,2,1,0:T(4,128)S(1)} collective-permute-done((f32[3,14,3,128]{3,2,1,0:T(4,128)S(1)}, f32[3,14,3,128]{3,2,1,0:T(4,128)S(1)}, u32[]{:S(2)}, u32[]{:S(2)}) %collective-permute-start.2) | collective-permute-done | bytes 64544 | tf_op jit(solution)/shard_map/ppermute | solution.py:22
  15.7 4.6 %collective-permute-done.3 = f32[3,14,3,128]{3,2,1,0:T(4,128)S(1)} collective-permute-done((f32[3,14,3,128]{3,2,1,0:T(4,128)S(1)}, f32[3,14,3,128]{3,2,1,0:T(4,128)S(1)}, u32[]{:S(2)}, u32[]{:S(2)}) %collective-permute-start.3) | collective-permute-done | bytes 64544 | tf_op jit(solution)/shard_map/ppermute | solution.py:23
  20.3 0.4 select_maximum_fusion
  20.7 0.1 bitcast_multiply_fusion.95
  20.9 0.1 bitcast_multiply_fusion.91
  21.3 2.9 %add_add_fusion = (f32[8,8,128]{2,1,0:T(8,128)S(1)}, f32[8,8,128]{2,1,0:T(8,128)S(1)}, f32[8,8,128]{2,1,0:T(8,128)S(1)}, f32[8,8,128]{2,1,0:T(8,128)S(1)}, f32[8...) fusion(f32[8,8,128]{2,1,0:T(8,128)S(1)} %get-tuple-element.156,, ...), kind=kLoop, calls=%fused_computation.2511 | loop fusion | flops 9846784 | bytes 11868160 | tf_op jit(solution)/shard_map/add | solution.py:123
  24.2 2.2 %fusion.693 = (f32[8,8,128]{2,1,0:T(8,128)S(1)}, f32[8,8,128]{2,1,0:T(8,128)S(1)}, f32[8,8,128]{2,1,0:T(8,128)S(1)}) fusion(f32[3,8,8,128]{3,2,1,0:T(8,128)S(1)} %select_select_fusion, f32[8,8,128]{2,1,0:T(8,128)S(1)} %get-tuple-element.156, f32[8,8,128]{2,1,0:T(8,128)S(1)} %get-tuple-element.154, f32[8,8,128]{2,1,0:T(8,128)S(1)} %get-tuple-element.148, ...), kind=kLoop, calls=%fused_computation.926 | loop fusion | flops 7086080 | bytes 4587520 | tf_op jit(solution)/shard_map/mul | solution.py:130
  26.4 2.0 %collective-permute-start.4 = (f32[3,8,128]{2,1,0:T(8,128)S(1)}, f32[3,8,128]{2,1,0:T(8,128)S(1)}, u32[]{:S(2)}, u32[]{:S(2)}) collective-permute-start(f32[3,8,128]{2,1,0:T(8,128)S(1)} %get-tuple-element.203), channel_id=1, source_target_pairs={{0,4},{4,8},{8,12},{12,16},{16,20},{20,24},{24,28},{1,5},{5,9},{9,... | collective-permute-start | bytes 36872 | tf_op jit(solution)/shard_map/ppermute | solution.py:22
  28.5 3.5 %collective-permute-start.6 = (f32[3,8,128]{2,1,0:T(8,128)S(1)}, f32[3,8,128]{2,1,0:T(8,128)S(1)}, u32[]{:S(2)}, u32[]{:S(2)}) collective-permute-start(f32[3,8,128]{2,1,0:T(8,128)S(1)} %get-tuple-element.204), channel_id=1, source_target_pairs={{4,0},{8,4},{12,8},{16,12},{20,16},{24,20},{28,24},{5,1},{9,5},{13... | collective-permute-start | bytes 36872 | tf_op jit(solution)/shard_map/ppermute | solution.py:23
  32.1 1.9 %collective-permute-start.5 = (f32[3,8,128]{2,1,0:T(8,128)S(1)}, f32[3,8,128]{2,1,0:T(8,128)S(1)}, u32[]{:S(2)}, u32[]{:S(2)}) collective-permute-start(f32[3,8,128]{2,1,0:T(8,128)S(1)} %get-tuple-element.205), channel_id=1, source_target_pairs={{0,4},{4,8},{8,12},{12,16},{16,20},{20,24},{24,28},{1,5},{5,9},{9,... | collective-permute-start | bytes 36872 | tf_op jit(solution)/shard_map/ppermute | solution.py:22
  34.0 3.6 %collective-permute-start.9 = (f32[3,8,128]{2,1,0:T(8,128)S(1)}, f32[3,8,128]{2,1,0:T(8,128)S(1)}, u32[]{:S(2)}, u32[]{:S(2)}) collective-permute-start(f32[3,8,128]{2,1,0:T(8,128)S(1)} %get-tuple-element.206), channel_id=1, source_target_pairs={{4,0},{8,4},{12,8},{16,12},{20,16},{24,20},{28,24},{5,1},{9,5},{13... | collective-permute-start | bytes 36872 | tf_op jit(solution)/shard_map/ppermute | solution.py:23
  37.7 2.5 %collective-permute-start.7 = (f32[14,3,128]{2,1,0:T(4,128)S(1)}, f32[14,3,128]{2,1,0:T(4,128)S(1)}, u32[]{:S(2)}, u32[]{:S(2)}) collective-permute-start(f32[14,3,128]{2,1,0:T(4,128)S(1)} %get-tuple-element.195), channel_id=1, source_target_pairs={{0,1},{1,2},{2,3},{4,5},{5,6},{6,7},{8,9},{9,10},{10,11},{12,13},{... | collective-permute-start | bytes 64520 | tf_op jit(solution)/shard_map/ppermute | solution.py:22
  40.2 3.3 %collective-permute-start.8 = (f32[14,3,128]{2,1,0:T(4,128)S(1)}, f32[14,3,128]{2,1,0:T(4,128)S(1)}, u32[]{:S(2)}, u32[]{:S(2)}) collective-permute-start(f32[14,3,128]{2,1,0:T(4,128)S(1)} %get-tuple-element.196), channel_id=1, source_target_pairs={{1,0},{2,1},{3,2},{5,4},{6,5},{7,6},{9,8},{10,9},{11,10},{13,12},{... | collective-permute-start | bytes 64520 | tf_op jit(solution)/shard_map/ppermute | solution.py:23
  43.6 3.4 %collective-permute-start.10 = (f32[14,3,128]{2,1,0:T(4,128)S(1)}, f32[14,3,128]{2,1,0:T(4,128)S(1)}, u32[]{:S(2)}, u32[]{:S(2)}) collective-permute-start(f32[14,3,128]{2,1,0:T(4,128)S(1)} %get-tuple-element.197), channel_id=1, source_target_pairs={{0,1},{1,2},{2,3},{4,5},{5,6},{6,7},{8,9},{9,10},{10,11},{12,13},{... | collective-permute-start | bytes 64520 | tf_op jit(solution)/shard_map/ppermute | solution.py:22
  47.0 2.4 %collective-permute-start.11 = (f32[14,3,128]{2,1,0:T(4,128)S(1)}, f32[14,3,128]{2,1,0:T(4,128)S(1)}, u32[]{:S(2)}, u32[]{:S(2)}) collective-permute-start(f32[14,3,128]{2,1,0:T(4,128)S(1)} %get-tuple-element.198), channel_id=1, source_target_pairs={{1,0},{2,1},{3,2},{5,4},{6,5},{7,6},{9,8},{10,9},{11,10},{13,12},{... | collective-permute-start | bytes 64520 | tf_op jit(solution)/shard_map/ppermute | solution.py:23
  49.5 0.2 select_maximum_fusion.6
  49.7 4.0 %collective-permute-done.11 = f32[14,3,128]{2,1,0:T(4,128)S(1)} collective-permute-done((f32[14,3,128]{2,1,0:T(4,128)S(1)}, f32[14,3,128]{2,1,0:T(4,128)S(1)}, u32[]{:S(2)}, u32[]{:S(2)}) %collective-permute-start.11) | collective-permute-done | bytes 21536 | tf_op jit(solution)/shard_map/ppermute | solution.py:23
  53.7 0.2 select_maximum_fusion.2
  53.9 0.1 fusion.482
  54.1 0.1 fusion.501
  54.3 2.5 %fusion.1549 = (f32[1,8,8,128]{3,2,1,0:T(8,128)S(1)}, f32[8,8,128]{2,1,0:T(8,128)S(1)}, f32[8,8,128]{2,1,0:T(8,128)S(1)}, f32[8,8,128]{2,1,0:T(8,128)S(1)}, f32[...) fusion(f32[8,8,128]{2,1,0:T(8,128)S(1)} %bitcast_divide_fusion,, ...), kind=kLoop, calls=%fused_computation.2632 | loop fusion | flops 10534912 | bytes 10502144 | tf_op jit(solution)/shard_map/stack | solution.py:151
  56.8 2.1 %fusion.1176 = f32[1,8,8,128]{3,2,1,0:T(8,128)S(1)} fusion(f32[8,8,128]{2,1,0:T(8,128)S(1)} %get-tuple-element.156, f32[8,8,128]{2,1,0:T(8,128)S(1)} %get-tuple-element.154, f32[8,8,128]{2,1,0:T(8,128)S(1)} %get-tuple-element.146, f32[8,8,128]{2,1,0:T(8,128)S(1)} %get-tuple-element.158, f32[8,8,128]{2,1,0:T(8,128)S(1)} %get-tuple-element.45, ...), kind=kLoop, calls=%fused_computation.1674 | loop fusion | flops 9068544 | bytes 8126464 | tf_op jit(solution)/shard_map/stack | solution.py:151
  58.9 2.0 %fusion.1164 = f32[1,8,8,128]{3,2,1,0:T(8,128)S(1)} fusion(f32[8,8,128]{2,1,0:T(8,128)S(1)} %get-tuple-element.154, f32[8,8,128]{2,1,0:T(8,128)S(1)} %get-tuple-element.158, f32[8,8,128]{2,1,0:T(8,128)S(1)} %get-tuple-element.50, f32[8,8,128]{2,1,0:T(8,128)S(1)} %get-tuple-element.49, f32[8,8,128]{2,1,0:T(8,128)S(1)} %get-tuple-element.48, ...), kind=kLoop, calls=%fused_computation.1651 | loop fusion | flops 9142272 | bytes 8159232 | tf_op jit(solution)/shard_map/stack | solution.py:151
  60.9 0.7 %multiply_add_fusion = (f32[3,8,8,128]{3,2,1,0:T(8,128)}, f32[3,8,8,128]{3,2,1,0:T(8,128)}) fusion(f32[3,8,8,128]{3,2,1,0:T(8,128)S(1)} %copy-done.1, f32[3,8,8,128]{3,2,1,0:T(8,128)S(1)} %copy-done.2, f32[8,8,128]{2,1,0:T(8,128)S(1)} %fusion.229, f32[1,8,8,128]{3,2,1,0:T(8,128)S(1)} %fusion.1164, f32[1,8,8,128]{3,2,1,0:T(8,128)S(1)} %fusion.1176, ...), kind=kLoop, calls=%fused_computation.94 | loop fusion | flops 147456 | bytes 524288 | tf_op jit(solution)/shard_map/add | solution.py:153
  (38 shorter events, 0.7 us)
Async XLA Ops:
  0.6 6.4 %copy-start.4 = (s32[8,8,128]{2,1,0:T(8,128)S(1)}, s32[8,8,128]{2,1,0:T(8,128)}, u32[]{:S(2)}) copy-start(s32[8,8,128]{2,1,0:T(8,128)} %param.7) | copy-start | bytes 98308
  1.4 6.6 %collective-permute-start = (f32[3,3,8,128]{3,2,1,0:T(8,128)S(1)}, f32[3,3,8,128]{3,2,1,0:T(8,128)S(1)}, u32[]{:S(2)}, u32[]{:S(2)}) collective-permute-start(f32[3,3,8,128]{3,2,1,0:T(8,128)S(1)} %get-tuple-element.190), channel_id=1, source_target_pairs={{0,4},{4,8},{8,12},{12,16},{16,20},{20,24},{24,28},{1,5},{5,9},{9,... | collective-permute-start | bytes 110600 | tf_op jit(solution)/shard_map/ppermute | solution.py:22
  3.4 5.5 %collective-permute-start.1 = (f32[3,3,8,128]{3,2,1,0:T(8,128)S(1)}, f32[3,3,8,128]{3,2,1,0:T(8,128)S(1)}, u32[]{:S(2)}, u32[]{:S(2)}) collective-permute-start(f32[3,3,8,128]{3,2,1,0:T(8,128)S(1)} %get-tuple-element.189), channel_id=1, source_target_pairs={{4,0},{8,4},{12,8},{16,12},{20,16},{24,20},{28,24},{5,1},{9,5},{13... | collective-permute-start | bytes 110600 | tf_op jit(solution)/shard_map/ppermute | solution.py:23
  7.0 0.7 %copy-start.3 = (f32[3,4]{1,0:T(4,128)S(1)}, f32[3,4]{1,0:T(4,128)}, u32[]{:S(2)}) copy-start(f32[3,4]{1,0:T(4,128)} %param.9) | copy-start | bytes 148
  7.9 0.9 %copy-start.1 = (f32[3,8,8,128]{3,2,1,0:T(8,128)S(1)}, f32[3,8,8,128]{3,2,1,0:T(8,128)}, u32[]{:S(2)}) copy-start(f32[3,8,8,128]{3,2,1,0:T(8,128)} %param.5) | copy-start | bytes 294916
  8.9 6.8 %collective-permute-start.2 = (f32[3,14,3,128]{3,2,1,0:T(4,128)S(1)}, f32[3,14,3,128]{3,2,1,0:T(4,128)S(1)}, u32[]{:S(2)}, u32[]{:S(2)}) collective-permute-start(f32[3,14,3,128]{3,2,1,0:T(4,128)S(1)} %get-tuple-element.184), channel_id=1, source_target_pairs={{0,1},{1,2},{2,3},{4,5},{5,6},{6,7},{8,9},{9,10},{10,11},{12,13},{... | collective-permute-start | bytes 193544 | tf_op jit(solution)/shard_map/ppermute | solution.py:22
  12.3 8.0 %collective-permute-start.3 = (f32[3,14,3,128]{3,2,1,0:T(4,128)S(1)}, f32[3,14,3,128]{3,2,1,0:T(4,128)S(1)}, u32[]{:S(2)}, u32[]{:S(2)}) collective-permute-start(f32[3,14,3,128]{3,2,1,0:T(4,128)S(1)} %get-tuple-element.185), channel_id=1, source_target_pairs={{1,0},{2,1},{3,2},{5,4},{6,5},{7,6},{9,8},{10,9},{11,10},{13,12},{... | collective-permute-start | bytes 193544 | tf_op jit(solution)/shard_map/ppermute | solution.py:23
  14.8 6.0 %copy-start = (s32[11,8,8,128]{3,2,1,0:T(8,128)S(1)}, s32[11,8,8,128]{3,2,1,0:T(8,128)}, u32[]{:S(2)}) copy-start(s32[11,8,8,128]{3,2,1,0:T(8,128)} %param.8) | copy-start | bytes 1081348
  26.4 11.2 %collective-permute-start.4 = (f32[3,8,128]{2,1,0:T(8,128)S(1)}, f32[3,8,128]{2,1,0:T(8,128)S(1)}, u32[]{:S(2)}, u32[]{:S(2)}) collective-permute-start(f32[3,8,128]{2,1,0:T(8,128)S(1)} %get-tuple-element.203), channel_id=1, source_target_pairs={{0,4},{4,8},{8,12},{12,16},{16,20},{20,24},{24,28},{1,5},{5,9},{9,... | collective-permute-start | bytes 36872 | tf_op jit(solution)/shard_map/ppermute | solution.py:22
  28.5 9.2 %collective-permute-start.6 = (f32[3,8,128]{2,1,0:T(8,128)S(1)}, f32[3,8,128]{2,1,0:T(8,128)S(1)}, u32[]{:S(2)}, u32[]{:S(2)}) collective-permute-start(f32[3,8,128]{2,1,0:T(8,128)S(1)} %get-tuple-element.204), channel_id=1, source_target_pairs={{4,0},{8,4},{12,8},{16,12},{20,16},{24,20},{28,24},{5,1},{9,5},{13... | collective-permute-start | bytes 36872 | tf_op jit(solution)/shard_map/ppermute | solution.py:23
  32.1 11.5 %collective-permute-start.5 = (f32[3,8,128]{2,1,0:T(8,128)S(1)}, f32[3,8,128]{2,1,0:T(8,128)S(1)}, u32[]{:S(2)}, u32[]{:S(2)}) collective-permute-start(f32[3,8,128]{2,1,0:T(8,128)S(1)} %get-tuple-element.205), channel_id=1, source_target_pairs={{0,4},{4,8},{8,12},{12,16},{16,20},{20,24},{24,28},{1,5},{5,9},{9,... | collective-permute-start | bytes 36872 | tf_op jit(solution)/shard_map/ppermute | solution.py:22
  34.0 9.6 %collective-permute-start.9 = (f32[3,8,128]{2,1,0:T(8,128)S(1)}, f32[3,8,128]{2,1,0:T(8,128)S(1)}, u32[]{:S(2)}, u32[]{:S(2)}) collective-permute-start(f32[3,8,128]{2,1,0:T(8,128)S(1)} %get-tuple-element.206), channel_id=1, source_target_pairs={{4,0},{8,4},{12,8},{16,12},{20,16},{24,20},{28,24},{5,1},{9,5},{13... | collective-permute-start | bytes 36872 | tf_op jit(solution)/shard_map/ppermute | solution.py:23
  37.7 11.8 %collective-permute-start.7 = (f32[14,3,128]{2,1,0:T(4,128)S(1)}, f32[14,3,128]{2,1,0:T(4,128)S(1)}, u32[]{:S(2)}, u32[]{:S(2)}) collective-permute-start(f32[14,3,128]{2,1,0:T(4,128)S(1)} %get-tuple-element.195), channel_id=1, source_target_pairs={{0,1},{1,2},{2,3},{4,5},{5,6},{6,7},{8,9},{9,10},{10,11},{12,13},{... | collective-permute-start | bytes 64520 | tf_op jit(solution)/shard_map/ppermute | solution.py:22
  40.2 9.3 %collective-permute-start.8 = (f32[14,3,128]{2,1,0:T(4,128)S(1)}, f32[14,3,128]{2,1,0:T(4,128)S(1)}, u32[]{:S(2)}, u32[]{:S(2)}) collective-permute-start(f32[14,3,128]{2,1,0:T(4,128)S(1)} %get-tuple-element.196), channel_id=1, source_target_pairs={{1,0},{2,1},{3,2},{5,4},{6,5},{7,6},{9,8},{10,9},{11,10},{13,12},{... | collective-permute-start | bytes 64520 | tf_op jit(solution)/shard_map/ppermute | solution.py:23
  43.6 6.1 %collective-permute-start.10 = (f32[14,3,128]{2,1,0:T(4,128)S(1)}, f32[14,3,128]{2,1,0:T(4,128)S(1)}, u32[]{:S(2)}, u32[]{:S(2)}) collective-permute-start(f32[14,3,128]{2,1,0:T(4,128)S(1)} %get-tuple-element.197), channel_id=1, source_target_pairs={{0,1},{1,2},{2,3},{4,5},{5,6},{6,7},{8,9},{9,10},{10,11},{12,13},{... | collective-permute-start | bytes 64520 | tf_op jit(solution)/shard_map/ppermute | solution.py:22
  47.0 6.7 %collective-permute-start.11 = (f32[14,3,128]{2,1,0:T(4,128)S(1)}, f32[14,3,128]{2,1,0:T(4,128)S(1)}, u32[]{:S(2)}, u32[]{:S(2)}) collective-permute-start(f32[14,3,128]{2,1,0:T(4,128)S(1)} %get-tuple-element.198), channel_id=1, source_target_pairs={{1,0},{2,1},{3,2},{5,4},{6,5},{7,6},{9,8},{10,9},{11,10},{13,12},{... | collective-permute-start | bytes 64520 | tf_op jit(solution)/shard_map/ppermute | solution.py:23
  58.9 2.0 %copy-start.2 = (f32[3,8,8,128]{3,2,1,0:T(8,128)S(1)}, f32[3,8,8,128]{3,2,1,0:T(8,128)}, u32[]{:S(2)}) copy-start(f32[3,8,8,128]{3,2,1,0:T(8,128)} %param.6) | copy-start | bytes 294916
where the time goes:
time: 62.1 us; the launch traced here: 61.6 us
  starting transfers between devices  34.2 us (55%)
  other arithmetic  14.2 us (23%)
  waiting for transfers between devices  9.53 us (15%)
  local copies, waits for them, and re-layouts  2.54 us (4%)
  between operations  1.09 us (2%)
    ppermute x6, starting transfers between devices, extended(): after = lax.ppermute(first, axis, down)  19 us
    ppermute x6, starting transfers between devices, extended(): before = lax.ppermute(last, axis, up)  15.2 us
    ppermute x6, waiting for transfers between devices, extended(): after = lax.ppermute(first, axis, down)  8.59 us
    another operation x3, other arithmetic, on_device(): force_sum = jnp.stack(force_parts)  6.5 us
    add x1, other arithmetic, on_device(): accumulated = accumulated + weighted  2.93 us
    mul x1, other arithmetic, on_device(): pressure_term = dilatation * pressure_ratio  2.18 us
    unnamed x11, local copies, waits for them, and re-layouts  1.44 us
  transfers between devices with their start and end apart: 12, of which 3 were waited for; matrix products, arithmetic and copies ran while one was open for 1% of the time, Pallas kernels for 0%

commit v1 on v0

v1 whole, which is shorter than its diff:
```python
import math

import jax
import jax.numpy as jnp
from jax import lax
from jax.experimental import pallas as pl
from jax.experimental.pallas import tpu as pltpu
from jax.sharding import PartitionSpec as P

HORIZON = 3
time_step = 0.3
bits_per_word = 12

MESH = pl.DeviceIdType.MESH
ROW_PAD = 8
DIRECTIONS = [(dx, dy) for dx in (-1, 0, 1) for dy in (-1, 0, 1) if (dx, dy) != (0, 0)]


def bond_offsets():
    listed = []
    for shift_x in range(-HORIZON, HORIZON + 1):
        for shift_y in range(-HORIZON, HORIZON + 1):
            for shift_z in range(-HORIZON, HORIZON + 1):
                radius = shift_x * shift_x + shift_y * shift_y + shift_z * shift_z
                if 0 < radius <= HORIZON * HORIZON:
                    listed.append((shift_x, shift_y, shift_z))
    return listed


OFFSETS = bond_offsets()
NUMBER = {offset: number for number, offset in enumerate(OFFSETS)}
PAIRS = sorted({(a, b) for a, b, c in OFFSETS})


def squared(offset):
    return offset[0] * offset[0] + offset[1] * offset[1] + offset[2] * offset[2]


def column(a, b):
    found = [(c, NUMBER[(a, b, c)]) for c in range(-HORIZON, HORIZON + 1) if (a, b, c) in NUMBER]
    return [(c, number, squared((a, b, c))) for c, number in found]


def scaled(x, factor):
    return x if factor == 1 else -x if factor == -1 else x * float(factor)


def plus(total, x, factor=1):
    if factor == 0:
        return total
    if total is None:
        return scaled(x, factor)
    if factor == 1:
        return total + x
    if factor == -1:
        return total - x
    return total + x * float(factor)


def ahead(x, c):
    if c == 0:
        return x
    length = x.shape[-1]
    return pltpu.roll(x, (-c) % length, x.ndim - 1)


def kernel(
    disp_hbm,
    region_hbm,
    words_hbm,
    moduli,
    accel,
    disp,
    shear,
    pressure,
    region,
    words,
    weight,
    term,
    ratio,
    inverse_mass,
    local_sem,
    send_sem,
    recv_sem,
):
    block_x, block_y = region.shape[0], region.shape[1]
    gx, gy = lax.axis_index("gx"), lax.axis_index("gy")
    size_x, size_y = lax.axis_size("gx"), lax.axis_size("gy")
    inner_x, inner_y = pl.ds(HORIZON, block_x), pl.ds(ROW_PAD, block_y)

    fetch_disp = pltpu.make_async_copy(disp_hbm, disp.at[:, inner_x, inner_y, :], local_sem.at[0])
    fetch_words = pltpu.make_async_copy(words_hbm, words, local_sem.at[1])
    fetch_region = pltpu.make_async_copy(region_hbm, region, local_sem.at[2])
    fetch_disp.start()
    fetch_words.start()
    fetch_region.start()

    def exists(dx, dy):
        fine = []
        if dx != 0:
            fine.append(gx > 0 if dx < 0 else gx < size_x - 1)
        if dy != 0:
            fine.append(gy > 0 if dy < 0 else gy < size_y - 1)
        return fine[0] if len(fine) == 1 else jnp.logical_and(fine[0], fine[1])

    barrier = pltpu.get_barrier_semaphore()
    for dx, dy in DIRECTIONS:

        @pl.when(exists(dx, dy))
        def _():
            pl.semaphore_signal(
                barrier,
                inc=1,
                device_id={"gx": gx + dx, "gy": gy + dy},
                device_id_type=MESH,
            )

    def clear(ref, lead):
        full_y = pl.ds(ROW_PAD - HORIZON, block_y + 2 * HORIZON)
        for side in (-1, 1):
            first_x = 0 if side < 0 else HORIZON + block_x
            first_y = ROW_PAD - HORIZON if side < 0 else ROW_PAD + block_y

            @pl.when(jnp.logical_not(exists(side, 0)))
            def _():
                where = lead + (pl.ds(first_x, HORIZON), full_y)
                ref[where] = jnp.zeros(ref.at[where].shape, jnp.float32)

            @pl.when(jnp.logical_not(exists(0, side)))
            def _():
                where = lead + (slice(None), pl.ds(first_y, HORIZON))
                ref[where] = jnp.zeros(ref.at[where].shape, jnp.float32)

    clear(disp, (slice(None),))
    clear(shear, ())
    clear(pressure, ())

    neighbours = (
        1 + (gx > 0).astype(jnp.int32) + (gx < size_x - 1).astype(jnp.int32)
    ) * (1 + (gy > 0).astype(jnp.int32) + (gy < size_y - 1).astype(jnp.int32)) - 1
    pl.semaphore_wait(barrier, neighbours)

    def copy_of(ref, lead, turn, place):
        dx, dy = DIRECTIONS[place]
        width = HORIZON if dx == 0 or dy == 0 else HORIZON - 1

        def span(step, base, length):
            if step == 0:
                return pl.ds(base, length), pl.ds(base, length)
            if step > 0:
                return pl.ds(base + length - width, width), pl.ds(base - width, width)
            return pl.ds(base, width), pl.ds(base + length, width)

        from_x, to_x = span(dx, HORIZON, block_x)
        from_y, to_y = span(dy, ROW_PAD, block_y)
        return pltpu.make_async_remote_copy(
            src_ref=ref.at[lead + (from_x, from_y)],
            dst_ref=ref.at[lead + (to_x, to_y)],
            send_sem=send_sem.at[turn, place],
            recv_sem=recv_sem.at[turn, place],
            device_id={"gx": gx + dx, "gy": gy + dy},
            device_id_type=MESH,
        )

    def send(ref, lead, turn):
        for place, (dx, dy) in enumerate(DIRECTIONS):

            @pl.when(exists(dx, dy))
            def _():
                copy_of(ref, lead, turn, place).start()

    def receive(ref, lead, turn):
        for place, (dx, dy) in enumerate(DIRECTIONS):

            @pl.when(exists(-dx, -dy))
            def _():
                copy_of(ref, lead, turn, place).wait_recv()

    def sent(ref, lead, turn):
        for place, (dx, dy) in enumerate(DIRECTIONS):

            @pl.when(exists(dx, dy))
            def _():
                copy_of(ref, lead, turn, place).wait_send()

    fetch_disp.wait()
    send(disp, (slice(None),), 0)

    fetch_words.wait()
    fetch_region.wait()

    def weigh(i, carry):
        by_length = {}
        for number, offset in enumerate(OFFSETS):
            bit = 1 << (number % bits_per_word)
            radius = squared(offset)
            intact = (words[number // bits_per_word, i] & bit) != 0
            value = jnp.where(intact, jnp.float32(1.0 / math.sqrt(radius)), jnp.float32(0.0))
            weight[number, i] = value
            by_length[radius] = plus(by_length.get(radius), value)
        volume = None
        for radius, total in by_length.items():
            volume = plus(volume, total, radius)
        here = region[i]
        fields = []
        for row in range(3):
            field = jnp.zeros(here.shape, jnp.float32)
            for material in range(moduli.shape[1]):
                field = jnp.where(here == material, moduli[row, material], field)
            fields.append(field)
        bulk_modulus, shear_modulus, density = fields
        inverse_volume = 1.0 / volume
        shear[i + HORIZON, inner_y] = 15.0 * shear_modulus * inverse_volume
        pressure_ratio = (3.0 * bulk_modulus - 5.0 * shear_modulus) * inverse_volume
        ratio[i] = 3.0 * pressure_ratio * inverse_volume
        inverse_mass[i] = 1.0 / density
        return carry

    lax.fori_loop(0, block_x, weigh, 0)
    send(shear, (), 1)

    receive(disp, (slice(None),), 0)

    def stretch(i, carry):
        centre = [disp[k, i + HORIZON, inner_y] for k in range(3)]
        total = None
        for a, b in PAIRS:
            rows = pl.ds(ROW_PAD + b, block_y)
            near = [disp[k, i + HORIZON + a, rows] for k in range(3)]
            flat_near, flat_here = None, None
            for k, factor in ((0, a), (1, b)):
                flat_near = plus(flat_near, near[k], factor)
                flat_here = plus(flat_here, centre[k], factor)
            for c, number, radius in column(a, b):
                along = ahead(plus(flat_near, near[2], c), c) - plus(flat_here, centre[2], c)
                part = weight[number, i] * along
                total = plus(total, part)
                term[number, i] = part if radius == 1 else part * (1.0 / radius)
        pressure[i + HORIZON, inner_y] = total * ratio[i]
        return carry

    lax.fori_loop(0, block_x, stretch, 0)
    send(pressure, (), 2)
    receive(shear, (), 1)

    def pull(i, carry):
        shear_here = shear[i + HORIZON, inner_y]
        pressure_here = pressure[i + HORIZON, inner_y]
        force = [None, None, None]
        for a, b in PAIRS:
            near = shear[i + HORIZON + a, pl.ds(ROW_PAD + b, block_y)]
            level = None
            for c, number, radius in column(a, b):
                part = weight[number, i] * pressure_here
                part = part + term[number, i] * (ahead(near, c) + shear_here)
                level = plus(level, part)
                force[2] = plus(force[2], part, c)
            force[0] = plus(force[0], level, a)
            force[1] = plus(force[1], level, b)
        for k in range(3):
            accel[k, i] = force[k]
        return carry

    lax.fori_loop(0, block_x, pull, 0)
    receive(pressure, (), 2)

    def push(i, carry):
        force = [accel[k, i] for k in range(3)]
        for a, b in PAIRS:
            near = pressure[i + HORIZON + a, pl.ds(ROW_PAD + b, block_y)]
            level = None
            for c, number, radius in column(a, b):
                part = weight[number, i] * ahead(near, c)
                level = plus(level, part)
                force[2] = plus(force[2], part, c)
            force[0] = plus(force[0], level, a)
            force[1] = plus(force[1], level, b)
        for k in range(3):
            accel[k, i] = force[k] * inverse_mass[i]
        return carry

    lax.fori_loop(0, block_x, push, 0)
    sent(disp, (slice(None),), 0)
    sent(shear, (), 1)
    sent(pressure, (), 2)


def on_device(displacement, velocity, region, bond_words, moduli):
    block = region.shape
    padded = (block[0] + 2 * HORIZON, block[1] + 2 * ROW_PAD, block[2])
    anywhere = pl.BlockSpec(memory_space=pl.ANY)
    bonds = len(OFFSETS)
    places = len(DIRECTIONS)
    acceleration = pl.pallas_call(
        kernel,
        out_shape=jax.ShapeDtypeStruct(displacement.shape, jnp.float32),
        in_specs=[anywhere] * 3 + [pl.BlockSpec(memory_space=pltpu.SMEM)],
        out_specs=pl.BlockSpec(memory_space=pltpu.VMEM),
        scratch_shapes=[
            pltpu.VMEM((3,) + padded, jnp.float32),
            pltpu.VMEM(padded, jnp.float32),
            pltpu.VMEM(padded, jnp.float32),
            pltpu.VMEM(block, jnp.int32),
            pltpu.VMEM(bond_words.shape, jnp.int32),
            pltpu.VMEM((bonds,) + block, jnp.float32),
            pltpu.VMEM((bonds,) + block, jnp.float32),
            pltpu.VMEM(block, jnp.float32),
            pltpu.VMEM(block, jnp.float32),
            pltpu.SemaphoreType.DMA((3,)),
            pltpu.SemaphoreType.DMA((3, places)),
            pltpu.SemaphoreType.DMA((3, places)),
        ],
        compiler_params=pltpu.CompilerParams(collective_id=0, has_side_effects=True),
        name="peridynamic",
    )(displacement, region, bond_words, moduli)
    new_velocity = velocity + time_step * acceleration
    return (displacement + time_step * new_velocity, new_velocity)


def solution(mesh):
    placed = (
        P(None, "gx", "gy", None),
        P(None, "gx", "gy", None),
        P("gx", "gy", None),
        P(None, "gx", "gy", None),
        P(),
    )
    return jax.shard_map(
        on_device,
        mesh=mesh,
        in_specs=placed,
        out_specs=(P(None, "gx", "gy", None), P(None, "gx", "gy", None)),
        check_vma=False,
    )
```

time: 62.1 us -> 17.8 us (0.29)
  the two profiles are of different devices: /device:TPU:10 before, /device:TPU:19 now
where the time goes in v1:
time: 17.8 us; the launch traced here: 17.6 us
  Pallas kernels  15.3 us (86%)
  other arithmetic  1.59 us (9%)
  between operations  0.67 us (4%)
    pallas_call x1, Pallas kernels, on_device(): pl.pallas_call(kernel, out_shape=jax.ShapeDtypeStruct(displacement.shape,...  15.3 us
    add x1, other arithmetic, on_device(): return (displacement + time_step * new_velocity, new_velocity)  1.59 us

profile of v1, /device:TPU:19, one launch (start us, length us, event | category | flops | bytes accessed | tf_op | source)
XLA Modules:
  0.0 17.6 jit_solution(2873094677716764899)
XLA Ops:
  0.6 0.0 copy-start
  0.6 0.0 copy-start.1
  0.7 15.3 %peridynamic.1 = f32[3,8,8,128]{3,2,1,0:T(8,128)} custom-call(f32[3,8,8,128]{3,2,1,0:T(8,128)} %disp_hbm.1, s32[8,8,128]{2,1,0:T(8,128)} %region_hbm.1, s32[11,8,8,128]{3,2,1,0:T(8,128)} %words_hbm.1, f32[3,4]{1,0:T(4,128)} %moduli.1), custom_call_target="tpu_custom_call" | custom-call | tf_op jit(solution)/shard_map/peridynamic/pallas_call | solution.py:294
  16.0 0.0 copy-done
  16.0 0.0 copy-done.1
  16.0 1.6 %multiply_add_fusion = (f32[3,8,8,128]{3,2,1,0:T(8,128)}, f32[3,8,8,128]{3,2,1,0:T(8,128)}) fusion(f32[3,8,8,128]{3,2,1,0:T(8,128)S(1)} %copy-done, f32[3,8,8,128]{3,2,1,0:T(8,128)S(1)} %copy-done.1, f32[3,8,8,128]{3,2,1,0:T(8,128)} %peridynamic.1), kind=kLoop, calls=%fused_computation | loop fusion | flops 98304 | bytes 491520 | tf_op jit(solution)/shard_map/add | solution.py:317
Async XLA Ops:
  0.6 15.3 %copy-start = (f32[3,8,8,128]{3,2,1,0:T(8,128)S(1)}, f32[3,8,8,128]{3,2,1,0:T(8,128)}, u32[]{:S(2)}) copy-start(f32[3,8,8,128]{3,2,1,0:T(8,128)} %disp_hbm.1) | copy-start | bytes 294916
  0.6 15.3 %copy-start.1 = (f32[3,8,8,128]{3,2,1,0:T(8,128)S(1)}, f32[3,8,8,128]{3,2,1,0:T(8,128)}, u32[]{:S(2)}) copy-start(f32[3,8,8,128]{3,2,1,0:T(8,128)} %param.6) | copy-start | bytes 294916

commit v2 on v1

--- a/solution.py
+++ b/solution.py
@@ -30,6 +30,11 @@
 OFFSETS = bond_offsets()
 NUMBER = {offset: number for number, offset in enumerate(OFFSETS)}
 PAIRS = sorted({(a, b) for a, b, c in OFFSETS})
+LEVEL = [(a, b) for a, b in PAIRS if b == 0]
+SLANTED = [(a, b) for a, b in PAIRS if b != 0]
+X_FACES = [place for place, (dx, dy) in enumerate(DIRECTIONS) if dy == 0]
+Y_FACES = [place for place, (dx, dy) in enumerate(DIRECTIONS) if dx == 0]
+CORNERS = [place for place, (dx, dy) in enumerate(DIRECTIONS) if dx != 0 and dy != 0]
 
 
 def squared(offset):
@@ -68,7 +73,7 @@
     disp_hbm,
     region_hbm,
     words_hbm,
-    moduli,
+    moduli_hbm,
     accel,
     disp,
     shear,
@@ -79,6 +84,8 @@
     term,
     ratio,
     inverse_mass,
+    partial,
+    moduli,
     local_sem,
     send_sem,
     recv_sem,
@@ -91,8 +98,10 @@
     fetch_disp = pltpu.make_async_copy(disp_hbm, disp.at[:, inner_x, inner_y, :], local_sem.at[0])
     fetch_words = pltpu.make_async_copy(words_hbm, words, local_sem.at[1])
     fetch_region = pltpu.make_async_copy(region_hbm, region, local_sem.at[2])
+    fetch_moduli = pltpu.make_async_copy(moduli_hbm, moduli, local_sem.at[3])
     fetch_disp.start()
     fetch_words.start()
+    fetch_moduli.start()
     fetch_region.start()
 
     def exists(dx, dy):
@@ -134,11 +143,6 @@
     clear(disp, (slice(None),))
     clear(shear, ())
     clear(pressure, ())
-
-    neighbours = (
-        1 + (gx > 0).astype(jnp.int32) + (gx < size_x - 1).astype(jnp.int32)
-    ) * (1 + (gy > 0).astype(jnp.int32) + (gy < size_y - 1).astype(jnp.int32)) - 1
-    pl.semaphore_wait(barrier, neighbours)
 
     def copy_of(ref, lead, turn, place):
         dx, dy = DIRECTIONS[place]
@@ -169,8 +173,9 @@
             def _():
                 copy_of(ref, lead, turn, place).start()
 
-    def receive(ref, lead, turn):
-        for place, (dx, dy) in enumerate(DIRECTIONS):
+    def receive(ref, lead, turn, places):
+        for place in places:
+            dx, dy = DIRECTIONS[place]
 
             @pl.when(exists(-dx, -dy))
             def _():
@@ -183,13 +188,28 @@
             def _():
                 copy_of(ref, lead, turn, place).wait_send()
 
-    fetch_disp.wait()
-    send(disp, (slice(None),), 0)
-
     fetch_words.wait()
     fetch_region.wait()
-
-    def weigh(i, carry):
+    fetch_moduli.wait()
+
+    def planes(body, first, count, step=2):
+        def both(j, carry):
+            body(first + step * j)
+            body(first + step * j + 1)
+            return carry
+
+        lax.fori_loop(0, count, both, 0)
+
+    def every(body):
+        planes(body, 0, block_x // 2)
+
+    def inner(body):
+        planes(body, 2, block_x // 2 - 2)
+
+    def outer(body):
+        planes(body, 0, 2, block_x - 2)
+
+    def weigh(i):
         by_length = {}
         for number, offset in enumerate(OFFSETS):
             bit = 1 << (number % bits_per_word)
@@ -214,17 +234,20 @@
         pressure_ratio = (3.0 * bulk_modulus - 5.0 * shear_modulus) * inverse_volume
         ratio[i] = 3.0 * pressure_ratio * inverse_volume
         inverse_mass[i] = 1.0 / density
-        return carry
-
-    lax.fori_loop(0, block_x, weigh, 0)
+
+    every(weigh)
+    fetch_disp.wait()
+    neighbours = (
+        1 + (gx > 0).astype(jnp.int32) + (gx < size_x - 1).astype(jnp.int32)
+    ) * (1 + (gy > 0).astype(jnp.int32) + (gy < size_y - 1).astype(jnp.int32)) - 1
+    pl.semaphore_wait(barrier, neighbours)
+
+    send(disp, (slice(None),), 0)
     send(shear, (), 1)
 
-    receive(disp, (slice(None),), 0)
-
-    def stretch(i, carry):
+    def stretch(i, pairs, total):
         centre = [disp[k, i + HORIZON, inner_y] for k in range(3)]
-        total = None
-        for a, b in PAIRS:
+        for a, b in pairs:
             rows = pl.ds(ROW_PAD + b, block_y)
             near = [disp[k, i + HORIZON + a, rows] for k in range(3)]
             flat_near, flat_here = None, None
@@ -236,14 +259,24 @@
                 part = weight[number, i] * along
                 total = plus(total, part)
                 term[number, i] = part if radius == 1 else part * (1.0 / radius)
-        pressure[i + HORIZON, inner_y] = total * ratio[i]
-        return carry
-
-    lax.fori_loop(0, block_x, stretch, 0)
+        return total
+
+    def stretch_level(i):
+        partial[i] = stretch(i, LEVEL, None)
+
+    def stretch_rest(i):
+        pressure[i + HORIZON, inner_y] = stretch(i, SLANTED, partial[i]) * ratio[i]
+
+    receive(disp, (slice(None),), 0, X_FACES)
+    every(stretch_level)
+    receive(disp, (slice(None),), 0, Y_FACES)
+    inner(stretch_rest)
+    receive(disp, (slice(None),), 0, CORNERS)
+    outer(stretch_rest)
     send(pressure, (), 2)
-    receive(shear, (), 1)
-
-    def pull(i, carry):
+    receive(shear, (), 1, X_FACES + Y_FACES + CORNERS)
+
+    def pull(i):
         shear_here = shear[i + HORIZON, inner_y]
         pressure_here = pressure[i + HORIZON, inner_y]
         force = [None, None, None]
@@ -259,14 +292,10 @@
             force[1] = plus(force[1], level, b)
         for k in range(3):
             accel[k, i] = force[k]
-        return carry
-
-    lax.fori_loop(0, block_x, pull, 0)
-    receive(pressure, (), 2)
-
-    def push(i, carry):
+
+    def push(i, pairs, mass):
         force = [accel[k, i] for k in range(3)]
-        for a, b in PAIRS:
+        for a, b in pairs:
             near = pressure[i + HORIZON + a, pl.ds(ROW_PAD + b, block_y)]
             level = None
             for c, number, radius in column(a, b):
@@ -276,10 +305,15 @@
             force[0] = plus(force[0], level, a)
             force[1] = plus(force[1], level, b)
         for k in range(3):
-            accel[k, i] = force[k] * inverse_mass[i]
-        return carry
-
-    lax.fori_loop(0, block_x, push, 0)
+            accel[k, i] = force[k] * inverse_mass[i] if mass else force[k]
+
+    every(pull)
+    receive(pressure, (), 2, X_FACES)
+    every(lambda i: push(i, LEVEL, False))
+    receive(pressure, (), 2, Y_FACES)
+    inner(lambda i: push(i, SLANTED, True))
+    receive(pressure, (), 2, CORNERS)
+    outer(lambda i: push(i, SLANTED, True))
     sent(disp, (slice(None),), 0)
     sent(shear, (), 1)
     sent(pressure, (), 2)
@@ -293,8 +327,8 @@
     places = len(DIRECTIONS)
     acceleration = pl.pallas_call(
         kernel,
-        out_shape=jax.ShapeDtypeStruct(displacement.shape, jnp.float32),
-        in_specs=[anywhere] * 3 + [pl.BlockSpec(memory_space=pltpu.SMEM)],
+        out_shape=pltpu.VMEM(displacement.shape, jnp.float32),
+        in_specs=[anywhere] * 4,
         out_specs=pl.BlockSpec(memory_space=pltpu.VMEM),
         scratch_shapes=[
             pltpu.VMEM((3,) + padded, jnp.float32),
@@ -306,7 +340,9 @@
             pltpu.VMEM((bonds,) + block, jnp.float32),
             pltpu.VMEM(block, jnp.float32),
             pltpu.VMEM(block, jnp.float32),
-            pltpu.SemaphoreType.DMA((3,)),
+            pltpu.VMEM(block, jnp.float32),
+            pltpu.SMEM(moduli.shape, jnp.float32),
+            pltpu.SemaphoreType.DMA((4,)),
             pltpu.SemaphoreType.DMA((3, places)),
             pltpu.SemaphoreType.DMA((3, places)),
         ],

time: 17.8 us -> 14.3 us (0.80)
  the two profiles are of different devices: /device:TPU:19 before, /device:TPU:5 now
where the time goes in v2:
time: 14.3 us; the launch traced here: 14.2 us
  Pallas kernels  12.8 us (90%)
  other arithmetic  0.7 us (5%)
  between operations  0.67 us (5%)
    pallas_call x1, Pallas kernels, on_device(): pl.pallas_call(kernel, out_shape=pltpu.VMEM(displacement.shape, jnp.float...  12.8 us
    add x1, other arithmetic, on_device(): return (displacement + time_step * new_velocity, new_velocity)  0.7 us

profile of v2, /device:TPU:5, one launch (start us, length us, event | category | flops | bytes accessed | tf_op | source)
XLA Modules:
  0.0 14.2 jit_solution(7461603738658106443)
XLA Ops:
  0.6 0.0 copy-start
  0.6 0.0 copy-start.1
  0.7 12.8 %peridynamic.1 = f32[3,8,8,128]{3,2,1,0:T(8,128)S(1)} custom-call(f32[3,8,8,128]{3,2,1,0:T(8,128)} %disp_hbm.1, s32[8,8,128]{2,1,0:T(8,128)} %region_hbm.1, s32[11,8,8,128]{3,2,1,0:T(8,128)} %words_hbm.1, f32[3,4]{1,0:T(4,128)} %moduli_hbm.1), custom_call_target="tpu_custom_call" | custom-call | tf_op jit(solution)/shard_map/peridynamic/pallas_call | solution.py:328
  13.5 0.0 copy-done
  13.5 0.0 copy-done.1
  13.5 0.7 %multiply_add_fusion = (f32[3,8,8,128]{3,2,1,0:T(8,128)}, f32[3,8,8,128]{3,2,1,0:T(8,128)}) fusion(f32[3,8,8,128]{3,2,1,0:T(8,128)S(1)} %copy-done, f32[3,8,8,128]{3,2,1,0:T(8,128)S(1)} %copy-done.1, f32[3,8,8,128]{3,2,1,0:T(8,128)S(1)} %peridynamic.1), kind=kLoop, calls=%fused_computation | loop fusion | flops 98304 | bytes 491520 | tf_op jit(solution)/shard_map/add | solution.py:353
Async XLA Ops:
  0.6 12.9 %copy-start = (f32[3,8,8,128]{3,2,1,0:T(8,128)S(1)}, f32[3,8,8,128]{3,2,1,0:T(8,128)}, u32[]{:S(2)}) copy-start(f32[3,8,8,128]{3,2,1,0:T(8,128)} %disp_hbm.1) | copy-start | bytes 294916
  0.6 12.9 %copy-start.1 = (f32[3,8,8,128]{3,2,1,0:T(8,128)S(1)}, f32[3,8,8,128]{3,2,1,0:T(8,128)}, u32[]{:S(2)}) copy-start(f32[3,8,8,128]{3,2,1,0:T(8,128)} %param.6) | copy-start | bytes 294916

commit v3 on v2

--- a/solution.py
+++ b/solution.py
@@ -85,6 +85,7 @@
     ratio,
     inverse_mass,
     partial,
+    turned,
     moduli,
     local_sem,
     send_sem,
@@ -267,6 +268,13 @@
     def stretch_rest(i):
         pressure[i + HORIZON, inner_y] = stretch(i, SLANTED, partial[i]) * ratio[i]
 
+    def turn(i):
+        for a, b in SLANTED:
+            for c, number, radius in column(a, b):
+                if c != 0:
+                    turned[number, i] = ahead(weight[number, i], -c)
+
+    every(turn)
     receive(disp, (slice(None),), 0, X_FACES)
     every(stretch_level)
     receive(disp, (slice(None),), 0, Y_FACES)
@@ -293,27 +301,52 @@
         for k in range(3):
             accel[k, i] = force[k]
 
-    def push(i, pairs, mass):
+    def push_level(i):
         force = [accel[k, i] for k in range(3)]
-        for a, b in pairs:
-            near = pressure[i + HORIZON + a, pl.ds(ROW_PAD + b, block_y)]
+        for a, b in LEVEL:
+            near = pressure[i + HORIZON + a, inner_y]
             level = None
             for c, number, radius in column(a, b):
                 part = weight[number, i] * ahead(near, c)
                 level = plus(level, part)
                 force[2] = plus(force[2], part, c)
             force[0] = plus(force[0], level, a)
-            force[1] = plus(force[1], level, b)
         for k in range(3):
-            accel[k, i] = force[k] * inverse_mass[i] if mass else force[k]
+            accel[k, i] = force[k]
+
+    def push_slanted(i):
+        force = [accel[k, i] for k in range(3)]
+        for c in range(-HORIZON, HORIZON + 1):
+            source = weight if c == 0 else turned
+            sums = [None, None, None]
+            for a in range(-HORIZON, HORIZON + 1):
+                row = None
+                for b in range(1, HORIZON + 1):
+                    if (a, b, c) in NUMBER:
+                        up, down = (
+                            source[NUMBER[(a, side, c)], i]
+                            * pressure[i + HORIZON + a, pl.ds(ROW_PAD + side, block_y)]
+                            for side in (b, -b)
+                        )
+                        row = plus(row, up + down)
+                        sums[1] = plus(sums[1], up - down, b)
+                if row is not None:
+                    sums[0] = plus(sums[0], row, a)
+                    sums[2] = plus(sums[2], row)
+            if sums[2] is not None:
+                for k, factor in ((0, 1), (1, 1), (2, c)):
+                    if factor != 0:
+                        force[k] = plus(force[k], ahead(sums[k], c), factor)
+        for k in range(3):
+            accel[k, i] = force[k] * inverse_mass[i]
 
     every(pull)
     receive(pressure, (), 2, X_FACES)
-    every(lambda i: push(i, LEVEL, False))
+    every(push_level)
     receive(pressure, (), 2, Y_FACES)
-    inner(lambda i: push(i, SLANTED, True))
+    inner(push_slanted)
     receive(pressure, (), 2, CORNERS)
-    outer(lambda i: push(i, SLANTED, True))
+    outer(push_slanted)
     sent(disp, (slice(None),), 0)
     sent(shear, (), 1)
     sent(pressure, (), 2)
@@ -341,6 +374,7 @@
             pltpu.VMEM(block, jnp.float32),
             pltpu.VMEM(block, jnp.float32),
             pltpu.VMEM(block, jnp.float32),
+            pltpu.VMEM((bonds,) + block, jnp.float32),
             pltpu.SMEM(moduli.shape, jnp.float32),
             pltpu.SemaphoreType.DMA((4,)),
             pltpu.SemaphoreType.DMA((3, places)),

time: 14.3 us -> 14.1 us (0.986)
  Pallas kernels: 12.8 us -> 12.6 us
    pallas_call x1, Pallas kernels: 12.8 us -> 12.6 us  [on_device(): pl.pallas_call(kernel, out_shape=pltpu.VMEM(displacement.shape, jnp.float...]
where the time goes in v3:
time: 14.1 us; the launch traced here: 14 us
  Pallas kernels  12.6 us (89%)
  other arithmetic  0.7 us (5%)
  between operations  0.67 us (5%)
    pallas_call x1, Pallas kernels, on_device(): pl.pallas_call(kernel, out_shape=pltpu.VMEM(displacement.shape, jnp.float...  12.6 us
    add x1, other arithmetic, on_device(): return (displacement + time_step * new_velocity, new_velocity)  0.7 us

profile of v3, /device:TPU:5, one launch (start us, length us, event | category | flops | bytes accessed | tf_op | source)
XLA Modules:
  0.0 14.0 jit_solution(14009263946471707437)
XLA Ops:
  0.6 0.0 copy-start
  0.6 0.0 copy-start.1
  0.7 12.6 %peridynamic.1 = f32[3,8,8,128]{3,2,1,0:T(8,128)S(1)} custom-call(f32[3,8,8,128]{3,2,1,0:T(8,128)} %disp_hbm.1, s32[8,8,128]{2,1,0:T(8,128)} %region_hbm.1, s32[11,8,8,128]{3,2,1,0:T(8,128)} %words_hbm.1, f32[3,4]{1,0:T(4,128)} %moduli_hbm.1), custom_call_target="tpu_custom_call" | custom-call | tf_op jit(solution)/shard_map/peridynamic/pallas_call | solution.py:361
  13.3 0.0 copy-done
  13.3 0.0 copy-done.1
  13.3 0.7 %multiply_add_fusion = (f32[3,8,8,128]{3,2,1,0:T(8,128)}, f32[3,8,8,128]{3,2,1,0:T(8,128)}) fusion(f32[3,8,8,128]{3,2,1,0:T(8,128)S(1)} %copy-done, f32[3,8,8,128]{3,2,1,0:T(8,128)S(1)} %copy-done.1, f32[3,8,8,128]{3,2,1,0:T(8,128)S(1)} %peridynamic.1), kind=kLoop, calls=%fused_computation | loop fusion | flops 98304 | bytes 491520 | tf_op jit(solution)/shard_map/add | solution.py:387
Async XLA Ops:
  0.6 12.6 %copy-start = (f32[3,8,8,128]{3,2,1,0:T(8,128)S(1)}, f32[3,8,8,128]{3,2,1,0:T(8,128)}, u32[]{:S(2)}) copy-start(f32[3,8,8,128]{3,2,1,0:T(8,128)} %disp_hbm.1) | copy-start | bytes 294916
  0.6 12.6 %copy-start.1 = (f32[3,8,8,128]{3,2,1,0:T(8,128)S(1)}, f32[3,8,8,128]{3,2,1,0:T(8,128)}, u32[]{:S(2)}) copy-start(f32[3,8,8,128]{3,2,1,0:T(8,128)} %param.6) | copy-start | bytes 294916

commit v4 on v3

--- a/solution.py
+++ b/solution.py
@@ -199,7 +199,10 @@
             body(first + step * j + 1)
             return carry
 
-        lax.fori_loop(0, count, both, 0)
+        if count == 2:
+            both(1, both(0, 0))
+        else:
+            lax.fori_loop(0, count, both, 0)
 
     def every(body):
         planes(body, 0, block_x // 2)

time: 14.1 us -> 13.9 us (0.986)
  Pallas kernels: 12.6 us -> 12.3 us
    pallas_call x1, Pallas kernels: 12.6 us -> 12.3 us  [on_device(): pl.pallas_call(kernel, out_shape=pltpu.VMEM(displacement.shape, jnp.float...]
where the time goes in v4:
time: 13.9 us; the launch traced here: 13.7 us
  Pallas kernels  12.3 us (88%)
  other arithmetic  0.7 us (5%)
  between operations  0.67 us (5%)
    pallas_call x1, Pallas kernels, on_device(): pl.pallas_call(kernel, out_shape=pltpu.VMEM(displacement.shape, jnp.float...  12.3 us
    add x1, other arithmetic, on_device(): return (displacement + time_step * new_velocity, new_velocity)  0.7 us

profile of v4, /device:TPU:5, one launch (start us, length us, event | category | flops | bytes accessed | tf_op | source)
XLA Modules:
  0.0 13.7 jit_solution(12045778184440349397)
XLA Ops:
  0.6 0.0 copy-start
  0.6 0.0 copy-start.1
  0.7 12.3 %peridynamic.1 = f32[3,8,8,128]{3,2,1,0:T(8,128)S(1)} custom-call(f32[3,8,8,128]{3,2,1,0:T(8,128)} %disp_hbm.1, s32[8,8,128]{2,1,0:T(8,128)} %region_hbm.1, s32[11,8,8,128]{3,2,1,0:T(8,128)} %words_hbm.1, f32[3,4]{1,0:T(4,128)} %moduli_hbm.1), custom_call_target="tpu_custom_call" | custom-call | tf_op jit(solution)/shard_map/peridynamic/pallas_call | solution.py:364
  13.0 0.0 copy-done
  13.0 0.0 copy-done.1
  13.0 0.7 %multiply_add_fusion = (f32[3,8,8,128]{3,2,1,0:T(8,128)}, f32[3,8,8,128]{3,2,1,0:T(8,128)}) fusion(f32[3,8,8,128]{3,2,1,0:T(8,128)S(1)} %copy-done, f32[3,8,8,128]{3,2,1,0:T(8,128)S(1)} %copy-done.1, f32[3,8,8,128]{3,2,1,0:T(8,128)S(1)} %peridynamic.1), kind=kLoop, calls=%fused_computation | loop fusion | flops 98304 | bytes 491520 | tf_op jit(solution)/shard_map/add | solution.py:390
Async XLA Ops:
  0.6 12.4 %copy-start = (f32[3,8,8,128]{3,2,1,0:T(8,128)S(1)}, f32[3,8,8,128]{3,2,1,0:T(8,128)}, u32[]{:S(2)}) copy-start(f32[3,8,8,128]{3,2,1,0:T(8,128)} %disp_hbm.1) | copy-start | bytes 294916
  0.6 12.4 %copy-start.1 = (f32[3,8,8,128]{3,2,1,0:T(8,128)S(1)}, f32[3,8,8,128]{3,2,1,0:T(8,128)}, u32[]{:S(2)}) copy-start(f32[3,8,8,128]{3,2,1,0:T(8,128)} %param.6) | copy-start | bytes 294916
